TPU v7x, 32 devices: a whole 2x2x4 slice. The times are simulated.
32 devices in a mesh: ctx: 8 (over z, y), mp: 4 (over x, core).
Axes of the slice: x: 2, y: 2, z: 4, core: 2. Of those that a mesh axis runs over, the one named last changes fastest.
Arguments:
- tokens: bfloat16 [3072, 6144], P('ctx', 'mp'), may hold values from -24 to 24, as said below
- qkv_weight: bfloat16 [6144, 3, 24, 128], P('ctx', None, 'mp'), may hold values from -1 to 1, as said below
Outputs:
- attended: bfloat16 [3072, 24, 128], P('ctx', 'mp')
Inputs may be any that keep to these rules, and one draw needn't show every extreme that they name: `tokens`: finite values. `qkv_weight`: entries lie within 8 / sqrt(6144) of zero.
All inputs are finite; a program needn't handle non-finite values.
Results may differ from a plain program's by a relative error of at most 0.0045.
The roundings to bfloat16 on the way count: a program that leaves them out, or rounds other values in their place, can miss the bound.
Values may be sent and summed in bfloat16 or wider, within the bound.
No kernel may reach another device: no remote copies, remote signals or barrier semaphores. Data moves between devices by JAX's collectives and lax.ppermute only.
A program may use at most 128 MiB of HBM per device.

v0:
```python
import math
import jax
import jax.numpy as jnp
from jax import lax
from jax.sharding import PartitionSpec as P

REACH = 4


def shifted(array, axis, by):
    devices = lax.axis_size(axis)
    return lax.ppermute(array, axis, [(i, (i + by) % devices) for i in range(devices)])


def collect_blocks(key_value):
    blocks = [key_value]
    current = key_value
    for step in range(1, REACH):
        current = shifted(current, "ctx", 1)
        blocks.append(current)
    return blocks


def on_device(tokens, qkv_weight):
    features = lax.all_gather(tokens, "mp", axis=1, tiled=True)
    rows_dev = features.shape[0]
    heads_local = qkv_weight.shape[2]
    head_size = qkv_weight.shape[3]
    scale = 1.0 / math.sqrt(head_size)
    piece = lax.all_gather(qkv_weight, "ctx", axis=0, tiled=True)
    flat_piece = piece.reshape(piece.shape[0], -1)
    full_total = jnp.dot(features, flat_piece, preferred_element_type=jnp.float32)
    projected = full_total.astype(jnp.bfloat16).reshape(rows_dev, 3, heads_local, head_size)
    queries = projected[:, 0]
    key_value = projected[:, 1:]
    blocks = collect_blocks(key_value)
    key_rows = jnp.concatenate([block[:, 0] for block in blocks], axis=0)
    value_rows = jnp.concatenate([block[:, 1] for block in blocks], axis=0)
    scores = (
        jnp.einsum("thd,shd->hts", queries, key_rows, preferred_element_type=jnp.float32) * scale
    )
    top = jnp.max(scores, axis=-1, keepdims=True)
    expo = jnp.exp(scores - top)
    totals = jnp.sum(expo, axis=-1, keepdims=True)
    probs = expo.astype(jnp.bfloat16)
    mixed = (
        jnp.einsum("hts,shd->htd", probs, value_rows, preferred_element_type=jnp.float32) / totals
    )
    return jnp.transpose(mixed, (1, 0, 2)).astype(jnp.bfloat16)


def solution(mesh):
    placed = (P("ctx", "mp"), P("ctx", None, "mp", None))
    return jax.shard_map(
        on_device, mesh=mesh, in_specs=placed, out_specs=P("ctx", "mp", None), check_vma=False
    )
```

profile of v0, /device:TPU:0, one launch (start us, length us, event | category | flops | bytes accessed | tf_op | source)
XLA Modules:
  0.0 727.5 jit_solution(14110665750935580521)
XLA Ops:
  6.5 0.0 all-gather.3.cloned.1.call-start
  6.5 0.7 all-gather.3.cloned.1.call-update
  7.3 0.0 all-gather.5.cloned.1.call-start
  7.3 6.1 copy.7
  13.4 0.0 all-gather.5.cloned.1.call-update
  13.4 35.7 %all-gather.3.cloned.1.call-done = bf16[384,6144]{1,0:T(8,128)(2,1)} async-done(((bf16[384,1536]{1,0:T(8,128)(2,1)}), bf16[384,6144]{1,0:T(8,128)(2,1)}) %all-gather.3.cloned.1.call-update) | async-done | bytes 4718608 | tf_op jit(solution)/shard_map/all_gather | solution.py:25
  49.1 541.0 %all-gather.5.cloned.1.call-done = bf16[6144,3,6,128]{0,3,2,1:T(8,128)(2,1)} async-done(((bf16[768,3,6,128]{0,3,2,1:T(8,128)(2,1)}), bf16[6144,3,6,128]{0,3,2,1:T(8,128)(2,1)}) %all-gather.5.cloned.1.call-update) | async-done | bytes 28311568 | tf_op jit(solution)/shard_map/all_gather | solution.py:30
  590.1 16.6 %convolution_convert_fusion = bf16[384,2304]{1,0:T(8,128)(2,1)S(1)} fusion(bf16[384,6144]{1,0:T(8,128)(2,1)} %all-gather.3.cloned.1.call-done, bf16[6144,2304]{0,1:T(8,128)(2,1)} %bitcast.35), kind=kOutput, calls=%fused_computation.7 | convolution fusion | flops 10872520704 | bytes 34799616 | tf_op jit(solution)/shard_map/dot_general | solution.py:32
  606.7 1.1 copy.8
  607.8 0.1 slice.44
  608.0 1.5 copy.15
  609.4 0.3 collective-permute-start
  609.8 30.3 %collective-permute-done = bf16[384,2,6,128]{3,0,2,1:T(8,128)(2,1)S(1)} collective-permute-done((bf16[384,2,6,128]{3,0,2,1:T(8,128)(2,1)}, bf16[384,2,6,128]{3,0,2,1:T(8,128)(2,1)S(1)}, u32[]{:S(2)}, u32[]{:S(2)}) %collective-permute-start) | collective-permute-done | bytes 1179680 | tf_op jit(solution)/shard_map/ppermute | solution.py:12
  640.0 0.0 copy-start
  640.0 0.0 collective-permute-start.1
  640.0 29.6 %collective-permute-done.1 = bf16[384,2,6,128]{3,0,2,1:T(8,128)(2,1)} collective-permute-done((bf16[384,2,6,128]{3,0,2,1:T(8,128)(2,1)S(1)}, bf16[384,2,6,128]{3,0,2,1:T(8,128)(2,1)}, u32[]{:S(2)}, u32[]{:S(2)}) %collective-permute-start.1) | collective-permute-done | bytes 1179680 | tf_op jit(solution)/shard_map/ppermute | solution.py:12
  669.7 0.0 copy-done
  669.7 0.0 collective-permute-start.2
  669.7 0.1 fusion.33
  669.8 0.3 copy.14
  670.1 0.3 copy.16
  670.4 1.3 slice_bitcast_fusion.5
  671.8 1.3 slice_bitcast_fusion.4
  673.1 25.5 %collective-permute-done.2 = bf16[384,2,6,128]{3,0,2,1:T(8,128)(2,1)} collective-permute-done((bf16[384,2,6,128]{3,0,2,1:T(8,128)(2,1)}, bf16[384,2,6,128]{3,0,2,1:T(8,128)(2,1)}, u32[]{:S(2)}, u32[]{:S(2)}) %collective-permute-start.2) | collective-permute-done | bytes 1179680 | tf_op jit(solution)/shard_map/ppermute | solution.py:12
  698.6 1.3 slice_bitcast_fusion.3
  699.9 6.2 multiply_reduce_fusion
  706.1 7.5 %fusion = f32[6,384]{1,0:T(8,128)S(1)} fusion(f32[6,384,1536]{2,1,0:T(8,128)} %get-tuple-element.14, f32[6,384]{1,0:T(8,128)S(1)} %get-tuple-element.13), kind=kLoop, calls=%fused_computation.2 | loop fusion | flops 10614528 | bytes 14174208 | tf_op jit(solution)/shard_map/reduce_sum | solution.py:44
  713.6 7.1 divide_convert_fusion
Async XLA Ops:
  6.5 42.6 %all-gather.3.cloned.1.call-start = ((), (), s32[]{:S(2)}) async-start(), calls=%async_computation | async-start | bytes 5898240 | tf_op jit(solution)/shard_map/all_gather | solution.py:25
  7.3 582.8 %all-gather.5.cloned.1.call-start = ((), (), s32[]{:S(2)}) async-start(), calls=%async_computation.1 | async-start | bytes 31850496 | tf_op jit(solution)/shard_map/all_gather | solution.py:30
  609.4 30.6 %collective-permute-start = (bf16[384,2,6,128]{3,0,2,1:T(8,128)(2,1)}, bf16[384,2,6,128]{3,0,2,1:T(8,128)(2,1)S(1)}, u32[]{:S(2)}, u32[]{:S(2)}) collective-permute-start(bf16[384,2,6,128]{3,0,2,1:T(8,128)(2,1)} %copy.15), channel_id=1, source_target_pairs={{0,4},{4,8},{8,12},{12,16},{16,20},{20,24},{24,28},{28,0},{1,5},{5... | collective-permute-start | bytes 3538952 | tf_op jit(solution)/shard_map/ppermute | solution.py:12
  640.0 29.6 %copy-start = (bf16[384,2,6,128]{3,0,2,1:T(8,128)(2,1)}, bf16[384,2,6,128]{3,0,2,1:T(8,128)(2,1)S(1)}, u32[]{:S(2)}) copy-start(bf16[384,2,6,128]{3,0,2,1:T(8,128)(2,1)S(1)} %collective-permute-done) | copy-start | bytes 3538948
  640.0 29.6 %collective-permute-start.1 = (bf16[384,2,6,128]{3,0,2,1:T(8,128)(2,1)S(1)}, bf16[384,2,6,128]{3,0,2,1:T(8,128)(2,1)}, u32[]{:S(2)}, u32[]{:S(2)}) collective-permute-start(bf16[384,2,6,128]{3,0,2,1:T(8,128)(2,1)S(1)} %collective-permute-done), channel_id=1, source_target_pairs={{0,4},{4,8},{8,12},{12,16},{16,20},{20,24},{24,28},{28,0},{1,5},{5... | collective-permute-start | bytes 3538952 | tf_op jit(solution)/shard_map/ppermute | solution.py:12
  669.7 28.9 %collective-permute-start.2 = (bf16[384,2,6,128]{3,0,2,1:T(8,128)(2,1)}, bf16[384,2,6,128]{3,0,2,1:T(8,128)(2,1)}, u32[]{:S(2)}, u32[]{:S(2)}) collective-permute-start(bf16[384,2,6,128]{3,0,2,1:T(8,128)(2,1)} %collective-permute-done.1), channel_id=1, source_target_pairs={{0,4},{4,8},{8,12},{12,16},{16,20},{20,24},{24,28},{28,0},{1,5},{5... | collective-permute-start | bytes 3538952 | tf_op jit(solution)/shard_map/ppermute | solution.py:12
Sparse Core Ops, SparseCore 0:
  8.9 40.1 all-gather.2
  50.6 539.4 all-gather.4
where the time goes:
time: 728 us
  waiting for transfers between devices  663 us (91%)
  matrix products  29.9 us (4%)
  local copies, waits for them, and re-layouts  13.4 us (2%)
  between operations  13.4 us (2%)
  other arithmetic  7.47 us (1%)
    all_gather x1, waiting for transfers between devices, on_device(): piece = lax.all_gather(qkv_weight, 'ctx', axis=0, tiled=True)  541 us
    ppermute x3, waiting for transfers between devices, shifted(): lax.ppermute(array, axis, [(i, (i + by) % devices) for i in range(devices)])  85.4 us
    all_gather x1, waiting for transfers between devices, on_device(): features = lax.all_gather(tokens, 'mp', axis=1, tiled=True)  35.7 us
    dot_general x1, matrix products, on_device(): jnp.dot(features, flat_piece, preferred_element_type=jnp.float32)  16.6 us
  transfers between devices with their start and end apart: 5, of which 5 were waited for; matrix products, arithmetic and copies ran while one was open for 1% of the time, Pallas kernels for 0%

commit v1 on v0

--- a/solution.py
+++ b/solution.py
@@ -5,6 +5,22 @@
 from jax.sharding import PartitionSpec as P
 
 REACH = 4
+
+
+def raise_the_things(sheet):
+    state_now = jax.lax.axis_size("ctx")
+    arr_next = jax.lax.axis_index("ctx")
+    near, z_new, v_now = (state_now, arr_next, sheet.shape[0])
+    found = tuple((p * near if k == 0 else p for k, p in enumerate(sheet.shape)))
+    r1 = lax.dynamic_update_slice_in_dim(
+        jnp.zeros(found, sheet.dtype), sheet, z_new * v_now, axis=0
+    )
+    for q in range(1, near):
+        sheet = jax.lax.ppermute(
+            sheet, "ctx", perm=tuple(((k, (k + 1) % near) for k in range(near)))
+        )
+        r1 = lax.dynamic_update_slice_in_dim(r1, sheet, (z_new - q) % near * v_now, axis=0)
+    return r1
 
 
 def shifted(array, axis, by):
@@ -27,7 +43,7 @@
     heads_local = qkv_weight.shape[2]
     head_size = qkv_weight.shape[3]
     scale = 1.0 / math.sqrt(head_size)
-    piece = lax.all_gather(qkv_weight, "ctx", axis=0, tiled=True)
+    piece = raise_the_things(qkv_weight)
     flat_piece = piece.reshape(piece.shape[0], -1)
     full_total = jnp.dot(features, flat_piece, preferred_element_type=jnp.float32)
     projected = full_total.astype(jnp.bfloat16).reshape(rows_dev, 3, heads_local, head_size)

time: 728 us -> 701 us (0.963)
  waiting for transfers between devices: 663 us -> 586 us
  local copies, waits for them, and re-layouts: 13.4 us -> 56.2 us
    all_gather x1 -> x0, waiting for transfers between devices: 541 us -> none  [on_device(): piece = lax.all_gather(qkv_weight, 'ctx', axis=0, tiled=True)]
    ppermute x0 -> x7, waiting for transfers between devices: none -> 515 us  [raise_the_things(): jax.lax.ppermute(sheet, 'ctx', perm=tuple(((k, (k + 1) % near) for k in r...]
    all_gather x1, waiting for transfers between devices: 35.7 us -> 0.01 us  [on_device(): features = lax.all_gather(tokens, 'mp', axis=1, tiled=True)]
    dynamic_update_slice x0 -> x8, local copies, waits for them, and re-layouts: none -> 23.4 us  [the longest x7 21.2 us: raise_the_things(): lax.dynamic_update_slice_in_dim(r1, sheet, (z_new - q) % near * v_now, ax...]
    ppermute x3, waiting for transfers between devices: 85.4 us -> 71 us  [shifted(): lax.ppermute(array, axis, [(i, (i + by) % devices) for i in range(devices)])]
    unnamed x6 -> x24, local copies, waits for them, and re-layouts: 8.14 us -> 18.9 us
    broadcast_in_dim x0 -> x1, local copies, waits for them, and re-layouts: none -> 9.63 us  [raise_the_things(): jnp.zeros(found, sheet.dtype)]
  transfers between devices with their start and end apart: 5 -> 11, of which waited for: 5 -> 10; matrix products, arithmetic and copies ran while one was open for 1% -> 5% of each run, Pallas kernels for 0% -> 0%
where the time goes in v1:
time: 701 us; the launch traced here: 700 us
  waiting for transfers between devices  586 us (84%)
  local copies, waits for them, and re-layouts  56.2 us (8%)
  matrix products  33.5 us (5%)
  between operations  13.5 us (2%)
  other arithmetic  7.53 us (1%)
    ppermute x7, waiting for transfers between devices, raise_the_things(): jax.lax.ppermute(sheet, 'ctx', perm=tuple(((k, (k + 1) % near) for k in r...  515 us
    ppermute x3, waiting for transfers between devices, shifted(): lax.ppermute(array, axis, [(i, (i + by) % devices) for i in range(devices)])  71 us
    dynamic_update_slice x7, local copies, waits for them, and re-layouts, raise_the_things(): lax.dynamic_update_slice_in_dim(r1, sheet, (z_new - q) % near * v_now, ax...  21.2 us
    dot_general x1, matrix products, on_device(): jnp.dot(features, flat_piece, preferred_element_type=jnp.float32)  20.2 us
    unnamed x24, local copies, waits for them, and re-layouts  18.9 us
  transfers between devices with their start and end apart: 11, of which 10 were waited for; matrix products, arithmetic and copies ran while one was open for 5% of the time, Pallas kernels for 0%

profile of v1, /device:TPU:0, one launch (start us, length us, event | category | flops | bytes accessed | tf_op | source)
XLA Modules:
  0.0 700.2 jit_solution(8765957279380406322)
XLA Ops:
  6.5 4.3 copy.7
  10.8 3.0 collective-permute-start
  13.8 79.6 %collective-permute-done = bf16[768,3,6,128]{0,3,2,1:T(8,128)(2,1)S(1)} collective-permute-done((bf16[768,3,6,128]{0,3,2,1:T(8,128)(2,1)S(1)}, bf16[768,3,6,128]{0,3,2,1:T(8,128)(2,1)S(1)}, u32[]{:S(2)}, u32[]{:S(2)}) %collective-permute-start) | collective-permute-done | bytes 3538976 | tf_op jit(solution)/shard_map/ppermute | solution.py:19
  93.4 1.7 copy-done
  95.1 80.4 %collective-permute-done.1 = bf16[768,3,6,128]{0,3,2,1:T(8,128)(2,1)S(1)} collective-permute-done((bf16[768,3,6,128]{0,3,2,1:T(8,128)(2,1)S(1)}, bf16[768,3,6,128]{0,3,2,1:T(8,128)(2,1)S(1)}, u32[]{:S(2)}, u32[]{:S(2)}) %collective-permute-start.1) | collective-permute-done | bytes 3538976 | tf_op jit(solution)/shard_map/ppermute | solution.py:19
  175.5 1.8 copy-done.2
  177.4 79.5 %collective-permute-done.2 = bf16[768,3,6,128]{0,3,2,1:T(8,128)(2,1)S(1)} collective-permute-done((bf16[768,3,6,128]{0,3,2,1:T(8,128)(2,1)S(1)}, bf16[768,3,6,128]{0,3,2,1:T(8,128)(2,1)S(1)}, u32[]{:S(2)}, u32[]{:S(2)}) %collective-permute-start.2) | collective-permute-done | bytes 3538976 | tf_op jit(solution)/shard_map/ppermute | solution.py:19
  256.9 1.8 copy-done.4
  258.7 78.6 %collective-permute-done.3 = bf16[768,3,6,128]{0,3,2,1:T(8,128)(2,1)S(1)} collective-permute-done((bf16[768,3,6,128]{0,3,2,1:T(8,128)(2,1)S(1)}, bf16[768,3,6,128]{0,3,2,1:T(8,128)(2,1)S(1)}, u32[]{:S(2)}, u32[]{:S(2)}) %collective-permute-start.3) | collective-permute-done | bytes 3538976 | tf_op jit(solution)/shard_map/ppermute | solution.py:19
  337.2 1.9 copy-done.6
  339.1 77.7 %collective-permute-done.4 = bf16[768,3,6,128]{0,3,2,1:T(8,128)(2,1)} collective-permute-done((bf16[768,3,6,128]{0,3,2,1:T(8,128)(2,1)S(1)}, bf16[768,3,6,128]{0,3,2,1:T(8,128)(2,1)}, u32[]{:S(2)}, u32[]{:S(2)}) %collective-permute-start.4) | collective-permute-done | bytes 3538976 | tf_op jit(solution)/shard_map/ppermute | solution.py:19
  416.9 77.0 %collective-permute-done.5 = bf16[768,3,6,128]{0,3,2,1:T(8,128)(2,1)} collective-permute-done((bf16[768,3,6,128]{0,3,2,1:T(8,128)(2,1)}, bf16[768,3,6,128]{0,3,2,1:T(8,128)(2,1)}, u32[]{:S(2)}, u32[]{:S(2)}) %collective-permute-start.5) | collective-permute-done | bytes 3538976 | tf_op jit(solution)/shard_map/ppermute | solution.py:19
  493.9 9.6 %broadcast_in_dim.2 = bf16[6144,3,6,128]{0,3,2,1:T(8,128)(2,1)} broadcast(bf16[]{:T(256)} %constant.59.clone.1), dimensions={} | broadcast | bytes 28311554 | tf_op jit(solution)/shard_map/broadcast_in_dim | solution.py:16
  503.5 2.2 constant_dynamic-update-slice_fusion.7
  506.8 2.0 constant_dynamic-update-slice_fusion.6
  510.1 2.2 constant_dynamic-update-slice_fusion.5
  513.4 2.0 constant_dynamic-update-slice_fusion.4
  516.6 2.3 constant_dynamic-update-slice_fusion.3
  519.0 4.3 constant_dynamic-update-slice_fusion.2
  523.2 4.1 constant_dynamic-update-slice_fusion.1
  527.4 42.7 %collective-permute-done.6 = bf16[768,3,6,128]{0,3,2,1:T(8,128)(2,1)} collective-permute-done((bf16[768,3,6,128]{0,3,2,1:T(8,128)(2,1)}, bf16[768,3,6,128]{0,3,2,1:T(8,128)(2,1)}, u32[]{:S(2)}, u32[]{:S(2)}) %collective-permute-start.6) | collective-permute-done | bytes 3538976 | tf_op jit(solution)/shard_map/ppermute | solution.py:19
  570.0 4.2 constant_dynamic-update-slice_fusion
  574.2 20.2 %convolution_convert_fusion = bf16[2304,384]{1,0:T(8,128)(2,1)S(1)} fusion(bf16[6144,2304]{0,1:T(8,128)(2,1)} %bitcast.31, bf16[384,6144]{1,0:T(8,128)(2,1)} %all-gather.2.cloned.1.call-done), kind=kOutput, calls=%fused_computation.7 | convolution fusion | flops 10872520704 | bytes 34799616 | tf_op jit(solution)/shard_map/dot_general | solution.py:48
  594.5 1.5 copy.15
  596.0 26.3 %collective-permute-done.7 = bf16[384,2,6,128]{3,0,2,1:T(8,128)(2,1)S(1)} collective-permute-done((bf16[384,2,6,128]{3,0,2,1:T(8,128)(2,1)}, bf16[384,2,6,128]{3,0,2,1:T(8,128)(2,1)S(1)}, u32[]{:S(2)}, u32[]{:S(2)}) %collective-permute-start.7) | collective-permute-done | bytes 1179680 | tf_op jit(solution)/shard_map/ppermute | solution.py:28
  622.3 25.9 %collective-permute-done.8 = bf16[384,2,6,128]{3,0,2,1:T(8,128)(2,1)} collective-permute-done((bf16[384,2,6,128]{3,0,2,1:T(8,128)(2,1)S(1)}, bf16[384,2,6,128]{3,0,2,1:T(8,128)(2,1)}, u32[]{:S(2)}, u32[]{:S(2)}) %collective-permute-start.8) | collective-permute-done | bytes 1179680 | tf_op jit(solution)/shard_map/ppermute | solution.py:28
  649.8 1.3 slice_bitcast_fusion.5
  651.1 1.3 slice_bitcast_fusion.4
  652.4 18.8 %collective-permute-done.9 = bf16[384,2,6,128]{3,0,2,1:T(8,128)(2,1)} collective-permute-done((bf16[384,2,6,128]{3,0,2,1:T(8,128)(2,1)}, bf16[384,2,6,128]{3,0,2,1:T(8,128)(2,1)}, u32[]{:S(2)}, u32[]{:S(2)}) %collective-permute-start.9) | collective-permute-done | bytes 1179680 | tf_op jit(solution)/shard_map/ppermute | solution.py:28
  672.5 6.2 multiply_reduce_fusion
  678.7 7.5 %fusion = f32[6,384]{1,0:T(8,128)S(1)} fusion(f32[6,384,1536]{2,1,0:T(8,128)} %get-tuple-element.14, f32[6,384]{1,0:T(8,128)S(1)} %get-tuple-element.13), kind=kLoop, calls=%fused_computation.2 | loop fusion | flops 10614528 | bytes 14174208 | tf_op jit(solution)/shard_map/reduce_sum | solution.py:60
  686.2 7.1 %divide_convert_fusion = bf16[384,6,128]{2,0,1:T(8,128)(2,1)} fusion(bf16[384,6,128]{2,0,1:T(8,128)(2,1)S(1)} %get-tuple-element.12, bf16[384,6,128]{2,0,1:T(8,128)(2,1)S(1)} %get-tuple-element.10, bf16[384,6,128]{2,0,1:T(8,128)(2,1)S(1)} %get-tuple-element.8, bf16[384,6,128]{2,0,1:T(8,128)(2,1)S(1)} %bitcast.36, f32[6,384,1536]{2,1,0:T(8,128)} %get-tuple-element.14, ...), kind=kOutput, calls=%fused_computation.24 | convolution fusion | flops 926613504 | bytes 17123328 | tf_op jit(solution)/shard_map/hts,shd->htd/dot_general | solution.py:63
  (33 shorter events, 7.5 us)
Async XLA Ops:
  6.5 567.6 %all-gather.2.cloned.1.call-start = ((), (), s32[]{:S(2)}) async-start(), calls=%async_computation | async-start | bytes 5898240 | tf_op jit(solution)/shard_map/all_gather | solution.py:41
  10.8 82.6 %collective-permute-start = (bf16[768,3,6,128]{0,3,2,1:T(8,128)(2,1)S(1)}, bf16[768,3,6,128]{0,3,2,1:T(8,128)(2,1)S(1)}, u32[]{:S(2)}, u32[]{:S(2)}) collective-permute-start(bf16[768,3,6,128]{0,3,2,1:T(8,128)(2,1)S(1)} %copy.7), channel_id=1, source_target_pairs={{0,4},{4,8},{8,12},{12,16},{16,20},{20,24},{24,28},{28,0},{1,5},{5... | collective-permute-start | bytes 10616840 | tf_op jit(solution)/shard_map/ppermute | solution.py:19
  93.4 1.7 copy-start
  95.1 80.4 %collective-permute-start.1 = (bf16[768,3,6,128]{0,3,2,1:T(8,128)(2,1)S(1)}, bf16[768,3,6,128]{0,3,2,1:T(8,128)(2,1)S(1)}, u32[]{:S(2)}, u32[]{:S(2)}) collective-permute-start(bf16[768,3,6,128]{0,3,2,1:T(8,128)(2,1)S(1)} %collective-permute-done), channel_id=1, source_target_pairs={{0,4},{4,8},{8,12},{12,16},{16,20},{20,24},{24,28},{28,0},{1,5},{5... | collective-permute-start | bytes 10616840 | tf_op jit(solution)/shard_map/ppermute | solution.py:19
  175.5 1.8 copy-start.2
  177.4 79.5 %collective-permute-start.2 = (bf16[768,3,6,128]{0,3,2,1:T(8,128)(2,1)S(1)}, bf16[768,3,6,128]{0,3,2,1:T(8,128)(2,1)S(1)}, u32[]{:S(2)}, u32[]{:S(2)}) collective-permute-start(bf16[768,3,6,128]{0,3,2,1:T(8,128)(2,1)S(1)} %collective-permute-done.1), channel_id=1, source_target_pairs={{0,4},{4,8},{8,12},{12,16},{16,20},{20,24},{24,28},{28,0},{1,5},{5... | collective-permute-start | bytes 10616840 | tf_op jit(solution)/shard_map/ppermute | solution.py:19
  256.9 1.8 copy-start.4
  258.7 78.6 %collective-permute-start.3 = (bf16[768,3,6,128]{0,3,2,1:T(8,128)(2,1)S(1)}, bf16[768,3,6,128]{0,3,2,1:T(8,128)(2,1)S(1)}, u32[]{:S(2)}, u32[]{:S(2)}) collective-permute-start(bf16[768,3,6,128]{0,3,2,1:T(8,128)(2,1)S(1)} %collective-permute-done.2), channel_id=1, source_target_pairs={{0,4},{4,8},{8,12},{12,16},{16,20},{20,24},{24,28},{28,0},{1,5},{5... | collective-permute-start | bytes 10616840 | tf_op jit(solution)/shard_map/ppermute | solution.py:19
  337.2 1.9 copy-start.6
  339.1 77.8 %collective-permute-start.4 = (bf16[768,3,6,128]{0,3,2,1:T(8,128)(2,1)S(1)}, bf16[768,3,6,128]{0,3,2,1:T(8,128)(2,1)}, u32[]{:S(2)}, u32[]{:S(2)}) collective-permute-start(bf16[768,3,6,128]{0,3,2,1:T(8,128)(2,1)S(1)} %collective-permute-done.3), channel_id=1, source_target_pairs={{0,4},{4,8},{8,12},{12,16},{16,20},{20,24},{24,28},{28,0},{1,5},{5... | collective-permute-start | bytes 10616840 | tf_op jit(solution)/shard_map/ppermute | solution.py:19
  416.9 77.0 %collective-permute-start.5 = (bf16[768,3,6,128]{0,3,2,1:T(8,128)(2,1)}, bf16[768,3,6,128]{0,3,2,1:T(8,128)(2,1)}, u32[]{:S(2)}, u32[]{:S(2)}) collective-permute-start(bf16[768,3,6,128]{0,3,2,1:T(8,128)(2,1)} %collective-permute-done.4), channel_id=1, source_target_pairs={{0,4},{4,8},{8,12},{12,16},{16,20},{20,24},{24,28},{28,0},{1,5},{5... | collective-permute-start | bytes 10616840 | tf_op jit(solution)/shard_map/ppermute | solution.py:19
  493.9 76.1 %collective-permute-start.6 = (bf16[768,3,6,128]{0,3,2,1:T(8,128)(2,1)}, bf16[768,3,6,128]{0,3,2,1:T(8,128)(2,1)}, u32[]{:S(2)}, u32[]{:S(2)}) collective-permute-start(bf16[768,3,6,128]{0,3,2,1:T(8,128)(2,1)} %collective-permute-done.5), channel_id=1, source_target_pairs={{0,4},{4,8},{8,12},{12,16},{16,20},{20,24},{24,28},{28,0},{1,5},{5... | collective-permute-start | bytes 10616840 | tf_op jit(solution)/shard_map/ppermute | solution.py:19
  503.5 3.3 copy-start.1
  506.8 3.3 copy-start.3
  510.1 3.3 copy-start.5
  513.4 3.3 copy-start.7
  596.0 26.3 %collective-permute-start.7 = (bf16[384,2,6,128]{3,0,2,1:T(8,128)(2,1)}, bf16[384,2,6,128]{3,0,2,1:T(8,128)(2,1)S(1)}, u32[]{:S(2)}, u32[]{:S(2)}) collective-permute-start(bf16[384,2,6,128]{3,0,2,1:T(8,128)(2,1)} %copy.15), channel_id=1, source_target_pairs={{0,4},{4,8},{8,12},{12,16},{16,20},{20,24},{24,28},{28,0},{1,5},{5... | collective-permute-start | bytes 3538952 | tf_op jit(solution)/shard_map/ppermute | solution.py:28
  622.3 25.9 %copy-start.8 = (bf16[384,2,6,128]{3,0,2,1:T(8,128)(2,1)}, bf16[384,2,6,128]{3,0,2,1:T(8,128)(2,1)S(1)}, u32[]{:S(2)}) copy-start(bf16[384,2,6,128]{3,0,2,1:T(8,128)(2,1)S(1)} %collective-permute-done.7) | copy-start | bytes 3538948
  622.3 25.9 %collective-permute-start.8 = (bf16[384,2,6,128]{3,0,2,1:T(8,128)(2,1)S(1)}, bf16[384,2,6,128]{3,0,2,1:T(8,128)(2,1)}, u32[]{:S(2)}, u32[]{:S(2)}) collective-permute-start(bf16[384,2,6,128]{3,0,2,1:T(8,128)(2,1)S(1)} %collective-permute-done.7), channel_id=1, source_target_pairs={{0,4},{4,8},{8,12},{12,16},{16,20},{20,24},{24,28},{28,0},{1,5},{5... | collective-permute-start | bytes 3538952 | tf_op jit(solution)/shard_map/ppermute | solution.py:28
  648.2 22.9 %collective-permute-start.9 = (bf16[384,2,6,128]{3,0,2,1:T(8,128)(2,1)}, bf16[384,2,6,128]{3,0,2,1:T(8,128)(2,1)}, u32[]{:S(2)}, u32[]{:S(2)}) collective-permute-start(bf16[384,2,6,128]{3,0,2,1:T(8,128)(2,1)} %collective-permute-done.8), channel_id=1, source_target_pairs={{0,4},{4,8},{8,12},{12,16},{16,20},{20,24},{24,28},{28,0},{1,5},{5... | collective-permute-start | bytes 3538952 | tf_op jit(solution)/shard_map/ppermute | solution.py:28
  678.7 7.5 %copy-start.9 = (bf16[384,1,6,128]{3,0,2,1:T(8,128)(2,1)S(1)}, bf16[384,1,6,128]{3,0,2,1:T(8,128)(2,1)}, u32[]{:S(2)}) copy-start(bf16[384,1,6,128]{3,0,2,1:T(8,128)(2,1)} %copy.16) | copy-start | bytes 1769476
Sparse Core Ops, SparseCore 0:
  417.0 38.1 all-gather.1
